TPU v7x, 32 devices: a whole 2x2x4 slice. The times are simulated.
32 devices in a mesh: groups: 2 (over x), branch: 2 (over core), sub: 8 (over z, y).
Axes of the slice: x: 2, y: 2, z: 4, core: 2. Of those that a mesh axis runs over, the one named last changes fastest.
Arguments:
- dispatch: float32 [128, 168, 2048], P(('groups', 'branch', 'sub')), parts along dimension 0, may hold values from 0 to 3
- multiplier: float32 [128, 48, 2048], P(('groups', 'branch', 'sub')), parts along dimension 0, may hold values from -3 to 3
- node_of: int32 [128], P(('groups', 'branch', 'sub')), parts along dimension 0, may hold values from 0 to 7, as said below
- prob_weight: int32 [128], P(('groups', 'branch', 'sub')), parts along dimension 0, may hold values from 1 to 16
- commitment: int32 [128, 168, 2048], P(('groups', 'branch', 'sub')), parts along dimension 0, may hold values 0 or 1
- zone_of: int32 [2048], replicated, may hold values from 0 to 31
- capacity: float32 [2048], replicated, may hold values from 0.5 to 4
- linear_cost: float32 [2048], replicated, may hold values from -0.5 to 1
- quad_cost: float32 [2048], replicated, may hold values from 0.5 to 2
- demand: float32 [128, 168, 32], P(('groups', 'branch', 'sub')), parts along dimension 0, may hold values from 19 to 64
Outputs:
- new_dispatch: float32 [128, 168, 2048], P(('groups', 'branch', 'sub')), parts along dimension 0
- new_multiplier: float32 [128, 48, 2048], P(('groups', 'branch', 'sub')), parts along dimension 0
- next_average: float32 [128, 48, 2048], P(('groups', 'branch', 'sub')), parts along dimension 0
- deviation: float32 [2], P('groups'), parts along dimension 0
There are 2 independent parts, one for each index of `groups`. A program takes and returns all parts, laid end to end along the dimension named above; an argument that names none is the same for every part. Nothing has to cross between parts.
Inputs may be any that keep to these rules, and one draw needn't show every extreme that they name: `node_of`: within each aligned block of 32 scenarios (one day-one branch), every node number holds exactly 4 scenarios.
All inputs are finite; a program needn't handle non-finite values. No bound on the sum of `commitment` on one device may be relied on, other than what follows from the above.
Results may differ from a plain program's by a relative error of at most 0.0001.
Values sent between devices are 32-bit elements; how exact they have to be, the bound alone decides.
A program may use at most 128 MiB of HBM per device.

v0:
```python
import jax
import jax.numpy as jnp
from jax import lax
from jax.sharding import PartitionSpec as P

DAY = 24
NODES_BR = 8
STEPS = 3
rho_value = 1.0
step_size = 0.3


def average(early_part, prob_weight, node_of, riding):
    weighting = prob_weight.astype(jnp.float32)
    scen_local = early_part.shape[0]
    gens = early_part.shape[2]
    member = (node_of[None, :] == jnp.arange(NODES_BR, dtype=jnp.int32)[:, None]).astype(
        jnp.float32
    )
    weighted = member * weighting[None, :]
    day_one = jnp.einsum(
        "s,stg->tg", weighting, early_part[:, :DAY], precision=lax.Precision.HIGHEST
    )
    weight_sum = jnp.sum(weighting)[None]
    day_two = jnp.einsum(
        "ks,stg->ktg", weighted, early_part[:, DAY:], precision=lax.Precision.HIGHEST
    )
    node_weight = jnp.sum(weighted, axis=1)
    day_two, node_weight = lax.psum((day_two, node_weight), "sub")
    day_one, weight_sum, riding = lax.psum((day_one, weight_sum, riding), ("branch", "sub"))
    root_mean = day_one / weight_sum[0]
    node_mean = day_two / node_weight[:, None, None]
    assigned = jnp.einsum("ks,ktg->stg", member, node_mean, precision=lax.Precision.HIGHEST)
    spread_root = jnp.broadcast_to(root_mean[None], (scen_local, DAY, gens))
    return (jnp.concatenate([spread_root, assigned], axis=1), weight_sum, riding)


def shards(
    dispatch,
    multiplier,
    node_of,
    prob_weight,
    commitment,
    zone_of,
    capacity,
    linear_cost,
    quad_cost,
    demand,
):
    section_hours = multiplier.shape[1]
    gens = zone_of.shape[0]
    zones_count = demand.shape[2]
    weighting = prob_weight.astype(jnp.float32)
    nothing = jnp.zeros((1,), jnp.float32)
    averages, weight_sum, unused = average(
        dispatch[:, :section_hours], prob_weight, node_of, nothing
    )
    spread_gap = dispatch[:, :section_hours] - averages
    local_spread = jnp.sum(weighting[:, None, None] * spread_gap * spread_gap)[None]
    dev_total = lax.psum(local_spread, ("branch", "sub"))
    new_multiplier = multiplier + rho_value * spread_gap
    zone_table = (zone_of[:, None] == jnp.arange(zones_count, dtype=jnp.int32)[None, :]).astype(
        jnp.float32
    )
    ceiling = capacity[None, None, :] * commitment.astype(jnp.float32)
    balance = zones_count / gens
    current = dispatch
    for sweep in range(STEPS):
        zone_sum = jnp.einsum("stg,gz->stz", current, zone_table, precision=lax.Precision.HIGHEST)
        mismatch = zone_sum - demand
        feedback = jnp.einsum("stz,gz->stg", mismatch, zone_table, precision=lax.Precision.HIGHEST)
        gradient = linear_cost + quad_cost * current + balance * feedback
        hedged = (
            gradient[:, :section_hours]
            + new_multiplier
            + rho_value * (current[:, :section_hours] - averages)
        )
        gradient = jnp.concatenate([hedged, gradient[:, section_hours:]], axis=1)
        current = jnp.clip(current - step_size * gradient, 0.0, ceiling)
    next_average, unused_sum, carried = average(
        current[:, :section_hours], prob_weight, node_of, nothing
    )
    deviation = dev_total / (weight_sum * section_hours * gens)
    return (current, new_multiplier, next_average, deviation)


def solution(mesh):
    in_specs = (
        P(("groups", "branch", "sub"), None, None),
        P(("groups", "branch", "sub"), None, None),
        P(("groups", "branch", "sub")),
        P(("groups", "branch", "sub")),
        P(("groups", "branch", "sub"), None, None),
        P(),
        P(),
        P(),
        P(),
        P(("groups", "branch", "sub"), None, None),
    )
    out_specs = (
        P(("groups", "branch", "sub"), None, None),
        P(("groups", "branch", "sub"), None, None),
        P(("groups", "branch", "sub"), None, None),
        P("groups"),
    )
    return jax.shard_map(shards, mesh=mesh, in_specs=in_specs, out_specs=out_specs, check_vma=False)
```

profile of v0, /device:TPU:0, one launch (start us, length us, event | category | flops | bytes accessed | tf_op | source)
XLA Modules:
  0.0 428.4 jit_solution(12756518674870253161)
XLA Ops:
  7.3 1.5 fusion.62
  8.8 2.5 fusion.25
  11.3 0.7 copy.33
  12.0 0.0 all-reduce.7.cloned.1.call-start
  12.1 0.7 convert_element_type.5
  12.7 4.0 fusion.23
  16.8 0.6 convert_reduce_fusion
  17.4 0.1 select_reduce_fusion
  17.5 35.9 %psum.56 = f32[1]{0:T(128)} all-reduce(f32[1]{0:T(128)} %bitcast.4), channel_id=1, replica_groups=mesh['groups'=2,'branch'=2,'sub'=8] {'branch','sub'}, use_global_device_ids=true, to_apply=%region_2.0 | all-reduce | flops 1 | bytes 8 | tf_op jit(solution)/shard_map/psum | solution.py:30
  53.4 17.6 %psum.58 = f32[8]{0:T(128)S(1)} all-reduce(f32[8]{0:T(128)S(1)} %select_reduce_fusion), channel_id=1, replica_groups=mesh['groups'=2,'branch'=2,'sub'=8] {'sub'}, use_global_device_ids=true, to_apply=%region_5.0 | all-reduce | flops 8 | bytes 64 | tf_op jit(solution)/shard_map/psum | solution.py:29
  71.1 5.7 %fusion.18 = f32[4,168,32]{1,2,0:T(8,128)S(1)} fusion(f32[4,168,32]{1,2,0:T(8,128)S(1)} %copy-done.6, f32[4,168,2048]{2,1,0:T(8,128)} %param.10, s32[2048]{0:T(1024)S(1)} %copy-done.7), kind=kOutput, calls=%fused_computation.36 | convolution fusion | flops 528569344 | bytes 5685248 | tf_op jit(solution)/shard_map/stg,gz->stz/dot_general | solution.py:69
  76.8 3.0 multiply_add_fusion.2
  79.8 2.4 copy-done.1
  82.2 22.3 %all-reduce.5.cloned.1.call-done = f32[24,2048]{1,0:T(8,128)} async-done(((f32[24,2048]{1,0:T(8,128)}), f32[24,2048]{1,0:T(8,128)}) %all-reduce.5.cloned.1.call-update) | async-done | bytes 196624 | tf_op jit(solution)/shard_map/psum | solution.py:30
  104.5 1.6 broadcast_divide_fusion.1
  106.1 90.5 %all-reduce.7.cloned.1.call-done = f32[8,24,2048]{2,0,1:T(8,128)} async-done(((f32[8,24,2048]{2,0,1:T(8,128)}), f32[8,24,2048]{2,0,1:T(8,128)}) %all-reduce.7.cloned.1.call-update) | async-done | bytes 1572880 | tf_op jit(solution)/shard_map/psum | solution.py:29
  196.5 2.5 fusion.16
  199.0 0.5 copy.14
  199.6 0.1 broadcast_in_dim.9
  199.7 2.9 fusion.12
  202.5 0.8 slice-done.4
  203.3 0.7 slice-done.1
  204.0 4.0 fusion.2
  208.0 3.0 convolution_subtract_fusion.1
  211.0 3.0 multiply_add_fusion.1
  214.1 0.4 slice.63
  214.5 0.5 fusion.11
  215.1 1.2 slice-done.2
  216.2 0.5 slice-done.3
  216.7 2.9 fusion.5
  219.6 3.0 convolution_subtract_fusion
  222.6 3.0 multiply_add_fusion
  225.6 0.5 fusion.10
  226.2 0.3 slice.66
  226.4 2.6 fusion.8
  229.1 2.4 copy-done.4
  231.5 0.1 fusion.61
  231.6 1.9 fusion.21
  233.5 0.7 copy.32
  234.3 3.3 fusion.19
  238.3 32.6 %psum.61 = f32[1]{0:T(128)} all-reduce(f32[1]{0:T(128)} %bitcast.10), channel_id=1, replica_groups=mesh['groups'=2,'branch'=2,'sub'=8] {'branch','sub'}, use_global_device_ids=true, to_apply=%region_9.10 | all-reduce | flops 1 | bytes 8 | tf_op jit(solution)/shard_map/psum | solution.py:60
  271.5 52.0 %all-reduce.9.cloned.1.call-done = f32[24,2048]{1,0:T(8,128)} async-done(((f32[24,2048]{1,0:T(8,128)}), f32[24,2048]{1,0:T(8,128)}) %all-reduce.9.cloned.1.call-update) | async-done | bytes 196624 | tf_op jit(solution)/shard_map/psum | solution.py:30
  323.6 1.6 broadcast_divide_fusion
  325.1 90.3 %all-reduce.11.cloned.1.call-done = f32[8,24,2048]{2,0,1:T(8,128)} async-done(((f32[8,24,2048]{2,0,1:T(8,128)}), f32[8,24,2048]{2,0,1:T(8,128)}) %all-reduce.11.cloned.1.call-update) | async-done | bytes 1572880 | tf_op jit(solution)/shard_map/psum | solution.py:29
  415.4 2.4 fusion.14
  417.8 0.2 broadcast_in_dim.10
  418.0 0.7 pad_maximum_fusion.1
  418.7 2.1 copy.15
  (39 shorter events, 0.3 us)
Async XLA Ops:
  7.2 9.6 %copy-start.11 = (s32[4]{0:T(128)S(1)}, s32[4]{0:T(128)}, u32[]{:S(2)}) copy-start(s32[4]{0:T(128)} %param.13) | copy-start | bytes 52
  7.2 10.2 %copy-start.12 = (s32[4]{0:T(128)S(1)}, s32[4]{0:T(128)}, u32[]{:S(2)}) copy-start(s32[4]{0:T(128)} %param.12) | copy-start | bytes 52
  7.2 63.9 %copy-start.7 = (s32[2048]{0:T(1024)S(1)}, s32[2048]{0:T(1024)}, u32[]{:S(2)}) copy-start(s32[2048]{0:T(1024)} %param.15) | copy-start | bytes 24580
  7.2 63.8 %copy-start.6 = (f32[4,168,32]{1,2,0:T(8,128)S(1)}, f32[4,168,32]{1,2,0:T(8,128)}, u32[]{:S(2)}) copy-start(f32[4,168,32]{1,2,0:T(8,128)} %param.19) | copy-start | bytes 258052
  7.2 97.3 %all-reduce.5.cloned.1.call-start = ((), (), s32[]{:S(2)}) async-start(), calls=%async_computation | async-start | bytes 393216 | tf_op jit(solution)/shard_map/psum | solution.py:30
  8.8 68.0 %copy-start.9 = (f32[2048]{0:T(1024)S(1)}, f32[2048]{0:T(1024)}, u32[]{:S(2)}) copy-start(f32[2048]{0:T(1024)} %param.18) | copy-start | bytes 24580
  8.8 68.0 %copy-start.10 = (f32[2048]{0:T(1024)S(1)}, f32[2048]{0:T(1024)}, u32[]{:S(2)}) copy-start(f32[2048]{0:T(1024)} %param.17) | copy-start | bytes 24580
  12.0 184.5 %all-reduce.7.cloned.1.call-start = ((), (), s32[]{:S(2)}) async-start(), calls=%async_computation.1 | async-start | bytes 3145728 | tf_op jit(solution)/shard_map/psum | solution.py:29
  16.7 306.8 %all-reduce.9.cloned.1.call-start = ((), (), s32[]{:S(2)}) async-start(), calls=%async_computation.2 | async-start | bytes 393216 | tf_op jit(solution)/shard_map/psum | solution.py:30
  71.0 5.7 %copy-start = (f32[4,168,2048]{2,1,0:T(8,128)S(1)}, f32[4,168,2048]{2,1,0:T(8,128)}, u32[]{:S(2)}) copy-start(f32[4,168,2048]{2,1,0:T(8,128)} %param.10) | copy-start | bytes 16515076
  79.8 2.4 copy-start.1
  82.2 117.4 %copy-start.5 = (f32[4,48,2048]{2,1,0:T(8,128)S(1)}, f32[4,48,2048]{2,1,0:T(8,128)}, u32[]{:S(2)}) copy-start(f32[4,48,2048]{2,1,0:T(8,128)} %param.11) | copy-start | bytes 4718596
  196.5 3.1 copy-start.2
  199.5 3.0 slice-start
  199.5 3.8 slice-start.4
  199.5 3.8 copy-start.8
  199.6 4.4 %slice-start.1 = ((s8[5505024]{0:T(1024)(128)(4,1)}), s8[1310720]{0:T(1024)(128)(4,1)S(1)}, s32[]{:S(2)}) async-start(s8[5505024]{0:T(1024)(128)(4,1)} %bitcast.41), calls=%async_computation.5 | async-start | bytes 2621440
  202.5 23.1 %copy-start.3 = (f32[4,48,2048]{2,1,0:T(8,128)}, f32[4,48,2048]{2,1,0:T(8,128)S(1)}, u32[]{:S(2)}) copy-start(f32[4,48,2048]{2,1,0:T(8,128)S(1)} %get-tuple-element.9) | copy-start | bytes 4718596
  214.0 2.2 slice-start.2
  214.5 2.2 slice-start.3
  229.1 2.4 copy-start.4
  234.3 181.1 %all-reduce.11.cloned.1.call-start = ((), (), s32[]{:S(2)}) async-start(), calls=%async_computation.3 | async-start | bytes 3145728 | tf_op jit(solution)/shard_map/psum | solution.py:29
Sparse Core Ops, SparseCore 0:
  12.1 92.3 all-reduce.4
  108.6 87.8 all-reduce.6
  234.4 89.0 all-reduce.8
  327.5 87.8 all-reduce.10
where the time goes:
time: 429 us; the launch traced here: 428 us
  waiting for transfers between devices  255 us (59%)
  blocking collectives  86.1 us (20%)
  matrix products  37.2 us (9%)
  other arithmetic  18.6 us (4%)
  between operations  16.5 us (4%)
  local copies, waits for them, and re-layouts  14.7 us (3%)
    psum x2, waiting for transfers between devices, average(): day_two, node_weight = lax.psum((day_two, node_weight), 'sub')  181 us
    psum x2, waiting for transfers between devices, average(): lax.psum((day_one, weight_sum, riding), ('branch', 'sub'))  74.3 us
    psum x1, blocking collectives, average(): lax.psum((day_one, weight_sum, riding), ('branch', 'sub'))  35.9 us
    psum x1, blocking collectives, shards(): dev_total = lax.psum(local_spread, ('branch', 'sub'))  32.6 us
    psum x1, blocking collectives, average(): day_two, node_weight = lax.psum((day_two, node_weight), 'sub')  17.6 us
    dot_general x3, matrix products, shards(): jnp.einsum('stg,gz->stz', current, zone_table, precision=lax.Precision.HI...  11.6 us
    min x3, other arithmetic, shards(): current = jnp.clip(current - step_size * gradient, 0.0, ceiling)  9.51 us
    unnamed x35, local copies, waits for them, and re-layouts  9.42 us
  transfers between devices with their start and end apart: 4, of which 4 were waited for; matrix products, arithmetic and copies ran while one was open for 5% of the time, Pallas kernels for 0%

commit v1 on v0

--- a/solution.py
+++ b/solution.py
@@ -57,7 +57,8 @@
     )
     spread_gap = dispatch[:, :section_hours] - averages
     local_spread = jnp.sum(weighting[:, None, None] * spread_gap * spread_gap)[None]
-    dev_total = lax.psum(local_spread, ("branch", "sub"))
+    blocks = lax.all_gather(local_spread, ("branch", "sub"), axis=0, tiled=False)
+    dev_total = blocks.sum(axis=0)
     new_multiplier = multiplier + rho_value * spread_gap
     zone_table = (zone_of[:, None] == jnp.arange(zones_count, dtype=jnp.int32)[None, :]).astype(
         jnp.float32

time: 429 us -> 429 us (level)
    psum x1 -> x0, blocking collectives: 32.6 us -> none  [shards(): dev_total = lax.psum(local_spread, ('branch', 'sub'))]
    unnamed x0 -> x1, blocking collectives: none -> 31.9 us
    unnamed x35 -> x40, local copies, waits for them, and re-layouts: 9.42 us -> 11.4 us
where the time goes in v1:
time: 429 us
  waiting for transfers between devices  253 us (59%)
  blocking collectives  85.4 us (20%)
  matrix products  37.2 us (9%)
  other arithmetic  19.1 us (4%)
  local copies, waits for them, and re-layouts  16.7 us (4%)
  between operations  16.5 us (4%)
    psum x2, waiting for transfers between devices, average(): day_two, node_weight = lax.psum((day_two, node_weight), 'sub')  181 us
    psum x2, waiting for transfers between devices, average(): lax.psum((day_one, weight_sum, riding), ('branch', 'sub'))  72.5 us
    psum x1, blocking collectives, average(): lax.psum((day_one, weight_sum, riding), ('branch', 'sub'))  35.9 us
    unnamed x1, blocking collectives  31.9 us
    psum x1, blocking collectives, average(): day_two, node_weight = lax.psum((day_two, node_weight), 'sub')  17.6 us
    dot_general x3, matrix products, shards(): jnp.einsum('stg,gz->stz', current, zone_table, precision=lax.Precision.HI...  11.6 us
    unnamed x40, local copies, waits for them, and re-layouts  11.4 us
    min x3, other arithmetic, shards(): current = jnp.clip(current - step_size * gradient, 0.0, ceiling)  9.51 us
  transfers between devices with their start and end apart: 4, of which 4 were waited for; matrix products, arithmetic and copies ran while one was open for 5% of the time, Pallas kernels for 0%

profile of v1, /device:TPU:0, one launch (start us, length us, event | category | flops | bytes accessed | tf_op | source)
XLA Modules:
  0.0 428.5 jit_solution(8918878337972799002)
XLA Ops:
  7.3 1.5 fusion.62
  8.8 2.5 fusion.25
  11.3 0.7 copy.33
  12.1 0.7 convert_element_type.5
  12.7 4.0 fusion.23
  16.8 0.6 convert_reduce_fusion
  17.5 35.9 %psum.49 = f32[1]{0:T(128)} all-reduce(f32[1]{0:T(128)} %bitcast.4), channel_id=1, replica_groups=mesh['groups'=2,'branch'=2,'sub'=8] {'branch','sub'}, use_global_device_ids=true, to_apply=%region_2.0 | all-reduce | flops 1 | bytes 8 | tf_op jit(solution)/shard_map/psum | solution.py:30
  53.4 17.6 %psum.51 = f32[8]{0:T(128)S(1)} all-reduce(f32[8]{0:T(128)S(1)} %select_reduce_fusion), channel_id=1, replica_groups=mesh['groups'=2,'branch'=2,'sub'=8] {'sub'}, use_global_device_ids=true, to_apply=%region_5.0 | all-reduce | flops 8 | bytes 64 | tf_op jit(solution)/shard_map/psum | solution.py:29
  71.0 5.7 %fusion.18 = f32[4,168,32]{1,2,0:T(8,128)S(1)} fusion(f32[4,168,32]{1,2,0:T(8,128)S(1)} %copy-done.6, f32[4,168,2048]{2,1,0:T(8,128)} %param.10, s32[2048]{0:T(1024)S(1)} %copy-done.7), kind=kOutput, calls=%fused_computation.36 | convolution fusion | flops 528569344 | bytes 5685248 | tf_op jit(solution)/shard_map/stg,gz->stz/dot_general | solution.py:70
  76.7 3.0 multiply_add_fusion.2
  79.7 2.4 copy-done.1
  82.2 22.3 %all-reduce.6.cloned.1.call-done = f32[24,2048]{1,0:T(8,128)} async-done(((f32[24,2048]{1,0:T(8,128)}), f32[24,2048]{1,0:T(8,128)}) %all-reduce.6.cloned.1.call-update) | async-done | bytes 196624 | tf_op jit(solution)/shard_map/psum | solution.py:30
  104.5 1.5 broadcast_divide_fusion.1
  106.0 90.5 %all-reduce.8.cloned.1.call-done = f32[8,24,2048]{2,0,1:T(8,128)} async-done(((f32[8,24,2048]{2,0,1:T(8,128)}), f32[8,24,2048]{2,0,1:T(8,128)}) %all-reduce.8.cloned.1.call-update) | async-done | bytes 1572880 | tf_op jit(solution)/shard_map/psum | solution.py:29
  196.6 2.5 fusion.16
  199.1 0.5 copy.14
  199.7 2.9 fusion.12
  202.5 0.8 slice-done.4
  203.3 0.7 slice-done.1
  204.1 4.0 fusion.2
  208.1 3.0 convolution_subtract_fusion.1
  211.1 3.0 multiply_add_fusion.1
  214.1 0.4 slice.63
  214.5 0.5 fusion.11
  215.1 1.2 slice-done.2
  216.3 0.5 slice-done.3
  216.8 2.9 fusion.5
  219.6 3.0 convolution_subtract_fusion
  222.6 3.0 multiply_add_fusion
  225.6 0.5 fusion.10
  226.2 0.3 slice.66
  226.5 2.6 fusion.8
  229.1 2.4 copy-done.4
  231.5 0.1 fusion.61
  231.7 1.9 fusion.21
  233.6 0.8 copy.32
  234.4 3.3 fusion.19
  237.8 0.6 dynamic-slice
  238.4 1.4 dynamic-update-slice
  240.3 31.9 %all-reduce = f32[16]{0:T(128)S(1)} all-reduce(f32[16]{0:T(128)S(1)} %dynamic-update-slice), channel_id=1, replica_groups=mesh['groups'=2,'branch'=2,'sub'=8] {'branch','sub'}, use_global_device_ids=true, to_apply=%add | all-reduce | flops 16 | bytes 128
  272.2 0.6 reduce.1
  273.5 50.2 %all-reduce.10.cloned.1.call-done = f32[24,2048]{1,0:T(8,128)} async-done(((f32[24,2048]{1,0:T(8,128)}), f32[24,2048]{1,0:T(8,128)}) %all-reduce.10.cloned.1.call-update) | async-done | bytes 196624 | tf_op jit(solution)/shard_map/psum | solution.py:30
  323.6 1.5 broadcast_divide_fusion
  325.1 90.4 %all-reduce.12.cloned.1.call-done = f32[8,24,2048]{2,0,1:T(8,128)} async-done(((f32[8,24,2048]{2,0,1:T(8,128)}), f32[8,24,2048]{2,0,1:T(8,128)}) %all-reduce.12.cloned.1.call-update) | async-done | bytes 1572880 | tf_op jit(solution)/shard_map/psum | solution.py:29
  415.5 2.4 fusion.14
  417.9 0.2 broadcast_in_dim.8
  418.1 0.7 pad_maximum_fusion.1
  418.8 2.1 copy.15
  (45 shorter events, 0.5 us)
Async XLA Ops:
  7.2 9.6 %copy-start.11 = (s32[4]{0:T(128)S(1)}, s32[4]{0:T(128)}, u32[]{:S(2)}) copy-start(s32[4]{0:T(128)} %param.13) | copy-start | bytes 52
  7.2 10.2 %copy-start.12 = (s32[4]{0:T(128)S(1)}, s32[4]{0:T(128)}, u32[]{:S(2)}) copy-start(s32[4]{0:T(128)} %param.12) | copy-start | bytes 52
  7.2 63.8 %copy-start.7 = (s32[2048]{0:T(1024)S(1)}, s32[2048]{0:T(1024)}, u32[]{:S(2)}) copy-start(s32[2048]{0:T(1024)} %param.15) | copy-start | bytes 24580
  7.2 63.8 %copy-start.6 = (f32[4,168,32]{1,2,0:T(8,128)S(1)}, f32[4,168,32]{1,2,0:T(8,128)}, u32[]{:S(2)}) copy-start(f32[4,168,32]{1,2,0:T(8,128)} %param.19) | copy-start | bytes 258052
  7.2 97.3 %all-reduce.6.cloned.1.call-start = ((), (), s32[]{:S(2)}) async-start(), calls=%async_computation | async-start | bytes 393216 | tf_op jit(solution)/shard_map/psum | solution.py:30
  8.8 67.9 %copy-start.9 = (f32[2048]{0:T(1024)S(1)}, f32[2048]{0:T(1024)}, u32[]{:S(2)}) copy-start(f32[2048]{0:T(1024)} %param.18) | copy-start | bytes 24580
  8.8 67.9 %copy-start.10 = (f32[2048]{0:T(1024)S(1)}, f32[2048]{0:T(1024)}, u32[]{:S(2)}) copy-start(f32[2048]{0:T(1024)} %param.17) | copy-start | bytes 24580
  12.0 184.5 %all-reduce.8.cloned.1.call-start = ((), (), s32[]{:S(2)}) async-start(), calls=%async_computation.1 | async-start | bytes 3145728 | tf_op jit(solution)/shard_map/psum | solution.py:29
  16.7 306.9 %all-reduce.10.cloned.1.call-start = ((), (), s32[]{:S(2)}) async-start(), calls=%async_computation.2 | async-start | bytes 393216 | tf_op jit(solution)/shard_map/psum | solution.py:30
  71.0 5.7 %copy-start = (f32[4,168,2048]{2,1,0:T(8,128)S(1)}, f32[4,168,2048]{2,1,0:T(8,128)}, u32[]{:S(2)}) copy-start(f32[4,168,2048]{2,1,0:T(8,128)} %param.10) | copy-start | bytes 16515076
  79.7 2.4 copy-start.1
  82.2 117.5 %copy-start.5 = (f32[4,48,2048]{2,1,0:T(8,128)S(1)}, f32[4,48,2048]{2,1,0:T(8,128)}, u32[]{:S(2)}) copy-start(f32[4,48,2048]{2,1,0:T(8,128)} %param.11) | copy-start | bytes 4718596
  196.6 3.1 copy-start.2
  199.5 3.0 slice-start
  199.5 3.8 slice-start.4
  199.6 3.8 copy-start.8
  199.7 4.4 %slice-start.1 = ((s8[5505024]{0:T(1024)(128)(4,1)}), s8[1310720]{0:T(1024)(128)(4,1)S(1)}, s32[]{:S(2)}) async-start(s8[5505024]{0:T(1024)(128)(4,1)} %bitcast.43), calls=%async_computation.5 | async-start | bytes 2621440
  202.5 23.1 %copy-start.3 = (f32[4,48,2048]{2,1,0:T(8,128)}, f32[4,48,2048]{2,1,0:T(8,128)S(1)}, u32[]{:S(2)}) copy-start(f32[4,48,2048]{2,1,0:T(8,128)S(1)} %get-tuple-element.9) | copy-start | bytes 4718596
  214.1 2.2 slice-start.2
  214.5 2.2 slice-start.3
  229.1 2.4 copy-start.4
  231.5 6.2 %copy-start.13 = (u32[32]{0:T(128)S(1)}, u32[32]{0:T(128)}, u32[]{:S(2)}) copy-start(u32[32]{0:T(128)} %constant.19) | copy-start | bytes 388
  234.3 181.2 %all-reduce.12.cloned.1.call-start = ((), (), s32[]{:S(2)}) async-start(), calls=%async_computation.3 | async-start | bytes 3145728 | tf_op jit(solution)/shard_map/psum | solution.py:29
Sparse Core Ops, SparseCore 0:
  12.1 92.3 all-reduce.5
  108.6 87.8 all-reduce.7
  234.5 89.1 all-reduce.9
  327.6 87.8 all-reduce.11
